TPU v7x, 512 devices: a whole 4x8x8 slice. The times are simulated.
512 devices in a mesh: fsdp: 32 (over z_lo, x, core), cp: 16 (over y, z_hi).
Axes of the slice: x: 4, y: 8, z: 8 (z_hi: 2, z_lo: 4; z = z_hi * 4 + z_lo), core: 2. Of those that a mesh axis runs over, the one named last changes fastest.
Arguments:
- queries: bfloat16 [4096, 16384], P('cp', 'fsdp'), may hold values from -8 to 8
- key_vectors: bfloat16 [4096, 1024], P(('fsdp', 'cp')), may hold values from -8 to 8
- value_vectors: bfloat16 [4096, 1024], P(('fsdp', 'cp')), may hold values from -6 to 6
- out_grads: bfloat16 [4096, 16384], P('cp', 'fsdp'), may hold values from -6 to 6
- pair_order: int32 [32], replicated, may hold values from 0 to 31, as said below
Outputs:
- attended: bfloat16 [4096, 16384], P('cp', 'fsdp')
- query_grads: bfloat16 [4096, 16384], P('cp', 'fsdp')
- key_grads: float32 [4096, 1024], P(('fsdp', 'cp'))
- value_grads: float32 [4096, 1024], P(('fsdp', 'cp'))
Inputs may be any that keep to these rules, and one draw needn't show every extreme that they name: `pair_order`: A permutation of the stretches; slots 2 c and 2 c + 1 hold stretches P and 31 - P for some P, in either order.
All inputs are finite; a program needn't handle non-finite values.
Results may differ from a plain program's by a relative error of at most 0.034.
Values may be sent and summed in bfloat16 or wider, within the bound.
No kernel may reach another device: no remote copies, remote signals or barrier semaphores. Data moves between devices by JAX's collectives and lax.ppermute only.
A program may use at most 64 MiB of HBM per device.

v0:
```python
import math
import jax
import jax.numpy as jnp
from jax import lax
from jax.sharding import PartitionSpec as P

HD = 128
NEG_FILL = -1e30


def block_scores(query_rows, key_part, positions, key_start, score_scale):
    scores = (
        jnp.einsum("nhd,jd->hnj", query_rows, key_part, preferred_element_type=jnp.float32)
        * score_scale
    )
    key_positions = key_start + jnp.arange(key_part.shape[0], dtype=jnp.int32)
    visible = key_positions[None, :] <= positions[:, None]
    return (scores, visible[None, :, :])


def attend(whole_k, whole_v, query_rows, positions, blocks, block_width):
    row_count, head_count, head_dim = query_rows.shape
    score_scale = 1.0 / math.sqrt(head_dim)

    def online_step(block_index, state_three):
        row_peak, row_total, value_sum = state_three
        key_start = block_index * block_width
        key_part = lax.dynamic_slice_in_dim(whole_k, key_start, block_width, 0)
        value_part = lax.dynamic_slice_in_dim(whole_v, key_start, block_width, 0)
        scores, visible = block_scores(query_rows, key_part, positions, key_start, score_scale)
        masked = jnp.where(visible, scores, NEG_FILL)
        new_peak = jnp.maximum(row_peak, jnp.max(masked, axis=2))
        factor = jnp.exp(row_peak - new_peak)
        weights = jnp.where(visible, jnp.exp(masked - new_peak[:, :, None]), 0.0)
        row_total = row_total * factor + jnp.sum(weights, axis=2)
        weight_half = weights.astype(jnp.bfloat16)
        block_sum = jnp.einsum(
            "hnj,jd->nhd", weight_half, value_part, preferred_element_type=jnp.float32
        )
        value_sum = value_sum * factor.T[:, :, None] + block_sum
        return (new_peak, row_total, value_sum)

    first_peak = jnp.full((head_count, row_count), NEG_FILL, jnp.float32)
    first_total = jnp.zeros((head_count, row_count), jnp.float32)
    first_sum = jnp.zeros((row_count, head_count, head_dim), jnp.float32)
    row_peak, row_total, value_sum = lax.fori_loop(
        0, blocks, online_step, (first_peak, first_total, first_sum)
    )
    log_total = row_peak + jnp.log(row_total)
    output = value_sum / row_total.T[:, :, None]
    return (output.astype(jnp.bfloat16), log_total)


def backprop(
    whole_k,
    whole_v,
    query_rows,
    grad_rows,
    positions,
    log_total,
    row_delta,
    blocks,
    block_width,
    key_acc,
    value_acc,
):
    row_count, head_count, head_dim = query_rows.shape
    score_scale = 1.0 / math.sqrt(head_dim)

    def grad_step(block_index, state_three):
        query_grad, key_sums, value_sums = state_three
        key_start = block_index * block_width
        key_part = lax.dynamic_slice_in_dim(whole_k, key_start, block_width, 0)
        value_part = lax.dynamic_slice_in_dim(whole_v, key_start, block_width, 0)
        scores, visible = block_scores(query_rows, key_part, positions, key_start, score_scale)
        prob_exact = jnp.where(visible, jnp.exp(scores - log_total[:, :, None]), 0.0)
        prob_half = prob_exact.astype(jnp.bfloat16)
        prob_grad = jnp.einsum(
            "nhd,jd->hnj", grad_rows, value_part, preferred_element_type=jnp.float32
        )
        score_grad = (prob_exact * (prob_grad - row_delta[:, :, None]) * score_scale).astype(
            jnp.bfloat16
        )
        query_grad = query_grad + jnp.einsum(
            "hnj,jd->nhd", score_grad, key_part, preferred_element_type=jnp.float32
        )
        key_term = jnp.einsum(
            "hnj,nhd->jd", score_grad, query_rows, preferred_element_type=jnp.float32
        )
        value_term = jnp.einsum(
            "hnj,nhd->jd", prob_half, grad_rows, preferred_element_type=jnp.float32
        )
        old_keys = lax.dynamic_slice_in_dim(key_sums, key_start, block_width, 0)
        old_values = lax.dynamic_slice_in_dim(value_sums, key_start, block_width, 0)
        key_sums = lax.dynamic_update_slice_in_dim(key_sums, old_keys + key_term, key_start, 0)
        value_sums = lax.dynamic_update_slice_in_dim(
            value_sums, old_values + value_term, key_start, 0
        )
        return (query_grad, key_sums, value_sums)

    first_grad = jnp.zeros((row_count, head_count, head_dim), jnp.float32)
    query_grad, key_acc, value_acc = lax.fori_loop(
        0, blocks, grad_step, (first_grad, key_acc, value_acc)
    )
    return (query_grad.astype(jnp.bfloat16), key_acc, value_acc)


def fetch_keys(key_vectors, value_vectors):
    fsdp_size = lax.axis_size("fsdp")
    kv_heads = key_vectors.shape[1] // HD
    repeats = fsdp_size // kv_heads
    rows_k, rows_v = (
        lax.all_gather(key_vectors, "cp", axis=0, tiled=True),
        lax.all_gather(value_vectors, "cp", axis=0, tiled=True),
    )
    gathered_rows = rows_k.shape[0]
    spread_k = jnp.repeat(rows_k.reshape(gathered_rows, kv_heads, HD), repeats, axis=1)
    spread_v = jnp.repeat(rows_v.reshape(gathered_rows, kv_heads, HD), repeats, axis=1)
    got_k, got_v = (
        lax.all_to_all(spread_k, "fsdp", split_axis=1, concat_axis=0, tiled=True),
        lax.all_to_all(spread_v, "fsdp", split_axis=1, concat_axis=0, tiled=True),
    )
    return (got_k.reshape(-1, HD), got_v.reshape(-1, HD))


def per_device(queries, key_vectors, value_vectors, out_grads, pair_order):
    tok_rows = queries.shape[0]
    q_heads = queries.shape[1] // HD
    kv_heads = key_vectors.shape[1] // HD
    half_rows = tok_rows // 2
    cp_size = lax.axis_size("cp")
    fsdp_size = lax.axis_size("fsdp")
    repeats = fsdp_size // kv_heads
    seq_len = tok_rows * cp_size
    block_width = math.gcd(256, seq_len)
    my_index = lax.axis_index("cp")
    first_stretch = pair_order[2 * my_index]
    second_stretch = pair_order[2 * my_index + 1]
    offsets = jnp.arange(tok_rows, dtype=jnp.int32)
    positions = jnp.where(
        offsets < half_rows,
        first_stretch * half_rows + offsets,
        second_stretch * half_rows + offsets - half_rows,
    )
    query_rows = queries.reshape(tok_rows, q_heads, HD)
    grad_rows = out_grads.reshape(tok_rows, q_heads, HD)
    whole_k, whole_v = fetch_keys(key_vectors, value_vectors)
    row_spans = ((0, tok_rows, jnp.maximum(first_stretch, second_stretch) + 1),)
    row_low, row_high, stretch_end = row_spans[0]
    blocks = (stretch_end * half_rows + block_width - 1) // block_width
    span_out, span_log = attend(whole_k, whole_v, query_rows, positions, blocks, block_width)
    row_delta = jnp.sum(grad_rows.astype(jnp.float32) * span_out.astype(jnp.float32), axis=2).T
    whole_k, whole_v = fetch_keys(key_vectors, value_vectors)
    key_acc = jnp.zeros((seq_len, HD), jnp.float32)
    value_acc = jnp.zeros((seq_len, HD), jnp.float32)
    span_grad, key_acc, value_acc = backprop(
        whole_k,
        whole_v,
        query_rows,
        grad_rows,
        positions,
        span_log,
        row_delta,
        blocks,
        block_width,
        key_acc,
        value_acc,
    )
    piece_rows = seq_len // fsdp_size
    term_k = key_acc.reshape(fsdp_size, piece_rows, HD)
    term_v = value_acc.reshape(fsdp_size, piece_rows, HD)
    got_k, got_v = (
        lax.all_to_all(
            term_k.astype(jnp.bfloat16), "fsdp", split_axis=0, concat_axis=0, tiled=True
        ).astype(term_k.dtype),
        lax.all_to_all(
            term_v.astype(jnp.bfloat16), "fsdp", split_axis=0, concat_axis=0, tiled=True
        ).astype(term_v.dtype),
    )
    summed_k = (
        got_k.reshape(kv_heads, repeats, piece_rows, HD)
        .sum(axis=1)
        .transpose(1, 0, 2)
        .reshape(piece_rows, kv_heads * HD)
    )
    summed_v = (
        got_v.reshape(kv_heads, repeats, piece_rows, HD)
        .sum(axis=1)
        .transpose(1, 0, 2)
        .reshape(piece_rows, kv_heads * HD)
    )
    final_k, final_v = (
        lax.psum_scatter(
            summed_k.astype(jnp.bfloat16), "cp", scatter_dimension=0, tiled=True
        ).astype(jnp.float32),
        lax.psum_scatter(
            summed_v.astype(jnp.bfloat16), "cp", scatter_dimension=0, tiled=True
        ).astype(jnp.float32),
    )
    attended = span_out.reshape(tok_rows, q_heads * HD)
    query_grads = span_grad.reshape(tok_rows, q_heads * HD)
    return (attended, query_grads, final_k, final_v)


def solution(mesh):
    return jax.shard_map(
        per_device,
        mesh=mesh,
        in_specs=(
            P("cp", "fsdp"),
            P(("fsdp", "cp"), None),
            P(("fsdp", "cp"), None),
            P("cp", "fsdp"),
            P(),
        ),
        out_specs=(
            P("cp", "fsdp"),
            P("cp", "fsdp"),
            P(("fsdp", "cp"), None),
            P(("fsdp", "cp"), None),
        ),
        check_vma=False,
    )
```

profile of v0, /device:TPU:4, one launch (start us, length us, event | category | flops | bytes accessed | tf_op | source)
XLA Modules:
  0.0 769.0 jit_solution(10527921880946531678)
XLA Ops:
  7.2 59.9 %all_gather.9 = bf16[128,1024]{1,0:T(8,128)(2,1)S(1)} all-gather(bf16[8,1024]{1,0:T(8,128)(2,1)} %param.11), channel_id=1, replica_groups=mesh['fsdp'=32,'cp'=16] {'cp'}, dimensions={0}, use_global_device_ids=true | all-gather | bytes 278528 | tf_op jit(solution)/shard_map/all_gather | solution.py:114
  67.1 1.2 broadcast_in_dim.54
  68.3 6.8 all-to-all-start.1
  75.2 62.8 %all_gather.8 = bf16[128,1024]{1,0:T(8,128)(2,1)S(1)} all-gather(bf16[8,1024]{1,0:T(8,128)(2,1)S(1)} %copy-done.6), channel_id=1, replica_groups=mesh['fsdp'=32,'cp'=16] {'cp'}, dimensions={0}, use_global_device_ids=true | all-gather | bytes 278528 | tf_op jit(solution)/shard_map/all_gather | solution.py:113
  138.0 1.2 broadcast_in_dim.53
  139.3 8.0 %all-to-all-start = ((bf16[128,32,128]{2,0,1:T(8,128)(2,1)}), bf16[128,32,128]{2,0,1:T(8,128)(2,1)S(1)}, u32[]{:S(2)}, u32[]{:S(2)}) async-start(bf16[128,32,128]{2,0,1:T(8,128)(2,1)} %bitcast.1), calls=%async_computation | async-start | bytes 2097152 | tf_op jit(solution)/shard_map/all_to_all | solution.py:120
  151.2 22.0 %all-to-all-done = bf16[128,32,128]{2,0,1:T(8,128)(2,1)S(1)} async-done(((bf16[128,32,128]{2,0,1:T(8,128)(2,1)}), bf16[128,32,128]{2,0,1:T(8,128)(2,1)S(1)}, u32[]{:S(2)}, u32[]{:S(2)}) %all-to-all-start) | async-done | bytes 1048608 | tf_op jit(solution)/shard_map/all_to_all | solution.py:120
  173.3 11.6 %while.30 = (s32[]{:T(128)}, f32[4,256]{1,0:T(4,128)S(1)}, f32[4,256]{1,0:T(4,128)S(1)}, f32[256,4,128]{0,2,1:T(8,128)S(1)}, s32[]{:T(128)}, /*index=5*/bf16[409...) while((s32[]{:T(128)}, f32[4,256]{1,0:T(4,128)S(1)}, ...), condition=%wide.region_3.4_spmd.clone, body=%wide.region_0.3_spmd.clone.sunk | while | flops 136909312 | bytes 4919495 | solution.py:46
  184.9 0.9 multiply_reduce_fusion
  186.5 1.5 broadcast.77
  187.9 57.6 %while.31 = (s32[]{:T(128)}, f32[256,4,128]{0,2,1:T(8,128)S(1)}, f32[4096,128]{1,0:T(8,128)}, f32[4096,128]{1,0:T(8,128)S(1)}, s32[]{:T(128)}, /*index=5*/bf16[4...) while((s32[]{:T(128)}, f32[256,4,128]{0,2,1:T(8,128)S(1)}, ...), condition=%wide.region_6.7_spmd.clone, body=%wide.region_5.6_spmd.clone.sunk | while | flops 337905152 | bytes 7680235 | solution.py:102
  188.1 1.2 fusion.94
  189.3 1.1 fusion.95
  190.4 1.1 fusion.96
  191.9 1.8 fusion.97
  193.8 1.2 fusion.94
  195.0 1.1 fusion.95
  196.2 1.1 fusion.96
  197.6 1.9 fusion.97
  199.6 1.2 fusion.94
  200.8 1.1 fusion.95
  202.0 1.1 fusion.96
  203.4 1.8 fusion.97
  205.3 1.2 fusion.94
  206.5 1.1 fusion.95
  207.7 1.1 fusion.96
  209.1 1.8 fusion.97
  211.1 1.2 fusion.94
  212.3 1.1 fusion.95
  213.5 1.1 fusion.96
  214.9 1.8 fusion.97
  216.8 1.2 fusion.94
  218.1 1.1 fusion.95
  219.2 1.1 fusion.96
  220.6 1.8 fusion.97
  222.6 1.2 fusion.94
  223.8 1.1 fusion.95
  225.0 1.1 fusion.96
  226.4 1.8 fusion.97
  228.3 1.2 fusion.94
  229.6 1.1 fusion.95
  230.7 1.1 fusion.96
  232.1 1.8 fusion.97
  234.1 1.2 fusion.94
  235.3 1.1 fusion.95
  236.5 1.1 fusion.96
  237.9 1.9 fusion.97
  239.9 1.2 fusion.94
  241.1 1.1 fusion.95
  242.2 1.1 fusion.96
  243.6 1.8 fusion.97
  245.5 1.1 convert_element_type.69
  246.6 6.0 all-to-all-start.3
  252.6 1.1 convert_element_type.63
  253.7 24.9 %all-to-all-done.3 = bf16[32,128,128]{2,1,0:T(8,128)(2,1)} async-done(((bf16[32,128,128]{2,1,0:T(8,128)(2,1)}), bf16[32,128,128]{2,1,0:T(8,128)(2,1)}, u32[]{:S(2)}, u32[]{:S(2)}) %all-to-all-start.3) | async-done | bytes 1048608 | tf_op jit(solution)/shard_map/all_to_all | solution.py:176
  278.6 5.8 all-to-all-start.2
  284.5 1.4 bitcast_reduce_fusion
  286.1 0.9 copy.85
  287.0 23.4 %all-to-all-done.2 = bf16[32,128,128]{2,1,0:T(8,128)(2,1)S(1)} async-done(((bf16[32,128,128]{2,1,0:T(8,128)(2,1)}), bf16[32,128,128]{2,1,0:T(8,128)(2,1)S(1)}, u32[]{:S(2)}, u32[]{:S(2)}) %all-to-all-start.2) | async-done | bytes 1048608 | tf_op jit(solution)/shard_map/all_to_all | solution.py:173
  310.7 0.8 copy.83
  313.3 227.3 %reduce-scatter.9.cloned.1.call-done = bf16[8,1024]{1,0:T(8,128)(2,1)} async-done(((bf16[128,1024]{1,0:T(8,128)(2,1)}), bf16[8,1024]{1,0:T(8,128)(2,1)}) %reduce-scatter.9.cloned.1.call-update) | async-done | bytes 16400
  540.5 0.9 copy.86
  542.2 218.4 %reduce-scatter.7.cloned.1.call-done = bf16[8,1024]{1,0:T(8,128)(2,1)} async-done(((bf16[128,1024]{1,0:T(8,128)(2,1)}), bf16[8,1024]{1,0:T(8,128)(2,1)}) %reduce-scatter.7.cloned.1.call-update) | async-done | bytes 16400
  760.6 0.9 copy.84
  (152 shorter events, 20.7 us)
Async XLA Ops:
  7.2 68.0 %copy-start.6 = (bf16[8,1024]{1,0:T(8,128)(2,1)S(1)}, bf16[8,1024]{1,0:T(8,128)(2,1)}, u32[]{:S(2)}) copy-start(bf16[8,1024]{1,0:T(8,128)(2,1)} %param.10) | copy-start | bytes 49156
  68.3 69.7 %all-to-all-start.1 = ((bf16[128,32,128]{2,0,1:T(8,128)(2,1)}), bf16[128,32,128]{2,0,1:T(8,128)(2,1)S(1)}, u32[]{:S(2)}, u32[]{:S(2)}) async-start(bf16[128,32,128]{2,0,1:T(8,128)(2,1)} %bitcast.6), calls=%async_computation.1 | async-start | bytes 2097152 | tf_op jit(solution)/shard_map/all_to_all | solution.py:121
  75.1 72.2 %copy-start.7 = (s32[32]{0:T(128)S(1)}, s32[32]{0:T(128)}, u32[]{:S(2)}) copy-start(s32[32]{0:T(128)} %param.13) | copy-start | bytes 388
  75.1 75.4 %copy-start.4 = (bf16[256,512]{1,0:T(8,128)(2,1)S(1)}, bf16[256,512]{1,0:T(8,128)(2,1)}, u32[]{:S(2)}) copy-start(bf16[256,512]{1,0:T(8,128)(2,1)} %param.12) | copy-start | bytes 786436
  138.0 12.8 %copy-start.5 = (bf16[256,512]{1,0:T(8,128)(2,1)S(1)}, bf16[256,512]{1,0:T(8,128)(2,1)}, u32[]{:S(2)}) copy-start(bf16[256,512]{1,0:T(8,128)(2,1)} %param.9) | copy-start | bytes 786436
  139.3 34.0 %all-to-all-start = ((bf16[128,32,128]{2,0,1:T(8,128)(2,1)}), bf16[128,32,128]{2,0,1:T(8,128)(2,1)S(1)}, u32[]{:S(2)}, u32[]{:S(2)}) async-start(bf16[128,32,128]{2,0,1:T(8,128)(2,1)} %bitcast.1), calls=%async_computation | async-start | bytes 2097152 | tf_op jit(solution)/shard_map/all_to_all | solution.py:120
  184.9 1.1 copy-start.1
  184.9 1.4 copy-start.2
  246.6 6.0 copy-start
  246.6 32.0 %all-to-all-start.3 = ((bf16[32,128,128]{2,1,0:T(8,128)(2,1)}), bf16[32,128,128]{2,1,0:T(8,128)(2,1)}, u32[]{:S(2)}, u32[]{:S(2)}) async-start(bf16[32,128,128]{2,1,0:T(8,128)(2,1)} %bitcast.152), calls=%async_computation.3 | async-start | bytes 2097152 | tf_op jit(solution)/shard_map/all_to_all | solution.py:176
  278.6 31.8 %all-to-all-start.2 = ((bf16[32,128,128]{2,1,0:T(8,128)(2,1)}), bf16[32,128,128]{2,1,0:T(8,128)(2,1)S(1)}, u32[]{:S(2)}, u32[]{:S(2)}) async-start(bf16[32,128,128]{2,1,0:T(8,128)(2,1)} %bitcast.151), calls=%async_computation.2 | async-start | bytes 2097152 | tf_op jit(solution)/shard_map/all_to_all | solution.py:173
  284.4 256.1 %reduce-scatter.9.cloned.1.call-start = ((), (), s32[]{:S(2)}) async-start(), calls=%async_computation.7 | async-start | bytes 278528
  285.9 25.7 %copy-start.3 = (bf16[256,4,128]{0,2,1:T(8,128)(2,1)S(1)}, bf16[256,4,128]{0,2,1:T(8,128)(2,1)}, u32[]{:S(2)}) copy-start(bf16[256,4,128]{0,2,1:T(8,128)(2,1)} %get-tuple-element.348) | copy-start | bytes 786436
  286.9 473.6 %reduce-scatter.7.cloned.1.call-start = ((), (), s32[]{:S(2)}) async-start(), calls=%async_computation.6 | async-start | bytes 278528
Sparse Core Ops, SparseCore 0:
  289.7 250.8 reduce-scatter.8
  545.0 215.5 reduce-scatter.6
where the time goes:
time: 772 us; the launch traced here: 769 us
  waiting for transfers between devices  516 us (67%)
  blocking collectives  123 us (16%)
  matrix products  63.5 us (8%)
  starting transfers between devices  26.8 us (3%)
  between operations  16.9 us (2%)
  local copies, waits for them, and re-layouts  12.9 us (2%)
  other arithmetic  9.22 us (1%)
    unnamed x4, waiting for transfers between devices  446 us
    all_gather x1, blocking collectives, fetch_keys(): lax.all_gather(key_vectors, 'cp', axis=0, tiled=True)  62.8 us
    all_gather x1, blocking collectives, fetch_keys(): lax.all_gather(value_vectors, 'cp', axis=0, tiled=True)  59.9 us
    all_to_all x1, waiting for transfers between devices, per_device(): lax.all_to_all(term_v.astype(jnp.bfloat16), 'fsdp', split_axis=0, concat_...  24.9 us
    all_to_all x1, waiting for transfers between devices, per_device(): lax.all_to_all(term_k.astype(jnp.bfloat16), 'fsdp', split_axis=0, concat_...  23.4 us
    all_to_all x1, waiting for transfers between devices, fetch_keys(): lax.all_to_all(spread_k, 'fsdp', split_axis=1, concat_axis=0, tiled=True)  22 us
    dot_general x10, matrix products, grad_step(): jnp.einsum('hnj,nhd->jd', score_grad, query_rows, preferred_element_type=...  18.5 us
    dot_general x20, matrix products, block_scores(): jnp.einsum('nhd,jd->hnj', query_rows, key_part, preferred_element_type=jn...  15.5 us
  transfers between devices with their start and end apart: 6, of which 5 were waited for; matrix products, arithmetic and copies ran while one was open for 1% of the time, Pallas kernels for 0%

commit v1 on v0

--- a/solution.py
+++ b/solution.py
@@ -110,7 +110,9 @@
     kv_heads = key_vectors.shape[1] // HD
     repeats = fsdp_size // kv_heads
     rows_k, rows_v = (
-        lax.all_gather(key_vectors, "cp", axis=0, tiled=True),
+        jnp.concatenate(
+            lax.all_to_all(jnp.stack([key_vectors] * lax.axis_size("cp")), "cp", 0, 0), axis=0
+        ),
         lax.all_gather(value_vectors, "cp", axis=0, tiled=True),
     )
     gathered_rows = rows_k.shape[0]

time: 772 us -> 749 us (0.970)
  blocking collectives: 123 us -> 55.4 us
  waiting for transfers between devices: 516 us -> 544 us
  starting transfers between devices: 26.8 us -> 40.9 us
    all_gather x1 -> x0, blocking collectives: 62.8 us -> none  [fetch_keys(): lax.all_gather(key_vectors, 'cp', axis=0, tiled=True)]
    all_to_all x1, waiting for transfers between devices: 0.01 us -> 25.8 us  [fetch_keys(): lax.all_to_all(spread_v, 'fsdp', split_axis=1, concat_axis=0, tiled=True)]
    all_to_all x0 -> x1, starting transfers between devices: none -> 15.6 us  [fetch_keys(): lax.all_to_all(jnp.stack([key_vectors] * lax.axis_size('cp')), 'cp', 0, 0)]
  transfers between devices with their start and end apart: 6 -> 7, of which waited for: 5 -> 6; matrix products, arithmetic and copies ran while one was open for 1% -> 1% of each run, Pallas kernels for 0% -> 0%
where the time goes in v1:
time: 749 us; the launch traced here: 746 us
  waiting for transfers between devices  544 us (73%)
  matrix products  63.6 us (8%)
  blocking collectives  55.4 us (7%)
  starting transfers between devices  40.9 us (5%)
  between operations  16.9 us (2%)
  local copies, waits for them, and re-layouts  14.4 us (2%)
  other arithmetic  9.22 us (1%)
    unnamed x4, waiting for transfers between devices  448 us
    all_gather x1, blocking collectives, fetch_keys(): lax.all_gather(value_vectors, 'cp', axis=0, tiled=True)  55.4 us
    all_to_all x1, waiting for transfers between devices, fetch_keys(): lax.all_to_all(spread_v, 'fsdp', split_axis=1, concat_axis=0, tiled=True)  25.8 us
    all_to_all x1, waiting for transfers between devices, per_device(): lax.all_to_all(term_v.astype(jnp.bfloat16), 'fsdp', split_axis=0, concat_...  24.9 us
    all_to_all x1, waiting for transfers between devices, per_device(): lax.all_to_all(term_k.astype(jnp.bfloat16), 'fsdp', split_axis=0, concat_...  23.4 us
    all_to_all x1, waiting for transfers between devices, fetch_keys(): lax.all_to_all(spread_k, 'fsdp', split_axis=1, concat_axis=0, tiled=True)  22 us
    dot_general x10, matrix products, grad_step(): jnp.einsum('hnj,nhd->jd', score_grad, query_rows, preferred_element_type=...  18.5 us
    all_to_all x1, starting transfers between devices, fetch_keys(): lax.all_to_all(jnp.stack([key_vectors] * lax.axis_size('cp')), 'cp', 0, 0)  15.6 us
  transfers between devices with their start and end apart: 7, of which 6 were waited for; matrix products, arithmetic and copies ran while one was open for 1% of the time, Pallas kernels for 0%

profile of v1, /device:TPU:4, one launch (start us, length us, event | category | flops | bytes accessed | tf_op | source)
XLA Modules:
  0.0 745.7 jit_solution(16475319339479097364)
XLA Ops:
  7.2 1.4 stack.2
  8.6 15.6 %all-to-all-start = ((bf16[16,8,1024]{2,1,0:T(8,128)(2,1)}), bf16[16,8,1024]{2,1,0:T(8,128)(2,1)S(1)}, u32[]{:S(2)}, u32[]{:S(2)}) async-start(bf16[16,8,1024]{2,1,0:T(8,128)(2,1)} %stack.2), calls=%async_computation | async-start | bytes 524288 | tf_op jit(solution)/shard_map/all_to_all | solution.py:114
  24.3 55.4 %all_gather.4 = bf16[128,1024]{1,0:T(8,128)(2,1)S(1)} all-gather(bf16[8,1024]{1,0:T(8,128)(2,1)} %param.11), channel_id=1, replica_groups=mesh['fsdp'=32,'cp'=16] {'cp'}, dimensions={0}, use_global_device_ids=true | all-gather | bytes 278528 | tf_op jit(solution)/shard_map/all_gather | solution.py:116
  79.7 1.2 broadcast_in_dim.54
  81.0 7.5 %all-to-all-start.2 = ((bf16[128,32,128]{2,0,1:T(8,128)(2,1)}), bf16[128,32,128]{2,0,1:T(8,128)(2,1)S(1)}, u32[]{:S(2)}, u32[]{:S(2)}) async-start(bf16[128,32,128]{2,0,1:T(8,128)(2,1)} %bitcast.6), calls=%async_computation.2 | async-start | bytes 2097152 | tf_op jit(solution)/shard_map/all_to_all | solution.py:123
  88.6 25.8 %all-to-all-done.2 = bf16[128,32,128]{2,0,1:T(8,128)(2,1)S(1)} async-done(((bf16[128,32,128]{2,0,1:T(8,128)(2,1)}), bf16[128,32,128]{2,0,1:T(8,128)(2,1)S(1)}, u32[]{:S(2)}, u32[]{:S(2)}) %all-to-all-start.2) | async-done | bytes 1048608 | tf_op jit(solution)/shard_map/all_to_all | solution.py:123
  114.4 1.2 broadcast_in_dim.53
  115.6 5.8 all-to-all-start.1
  125.3 22.0 %all-to-all-done.1 = bf16[128,32,128]{2,0,1:T(8,128)(2,1)S(1)} async-done(((bf16[128,32,128]{2,0,1:T(8,128)(2,1)}), bf16[128,32,128]{2,0,1:T(8,128)(2,1)S(1)}, u32[]{:S(2)}, u32[]{:S(2)}) %all-to-all-start.1) | async-done | bytes 1048608 | tf_op jit(solution)/shard_map/all_to_all | solution.py:122
  147.4 11.6 %while.30 = (s32[]{:T(128)}, f32[4,256]{1,0:T(4,128)S(1)}, f32[4,256]{1,0:T(4,128)S(1)}, f32[256,4,128]{0,2,1:T(8,128)S(1)}, s32[]{:T(128)}, /*index=5*/bf16[409...) while((s32[]{:T(128)}, f32[4,256]{1,0:T(4,128)S(1)}, ...), condition=%wide.region_3.4_spmd.clone, body=%wide.region_0.3_spmd.clone.sunk | while | flops 136909312 | bytes 4919495 | solution.py:46
  159.0 0.9 multiply_reduce_fusion
  160.6 1.5 broadcast.79
  162.1 57.6 %while.31 = (s32[]{:T(128)}, f32[256,4,128]{0,2,1:T(8,128)S(1)}, f32[4096,128]{1,0:T(8,128)}, f32[4096,128]{1,0:T(8,128)S(1)}, s32[]{:T(128)}, /*index=5*/bf16[4...) while((s32[]{:T(128)}, f32[256,4,128]{0,2,1:T(8,128)S(1)}, ...), condition=%wide.region_6.7_spmd.clone, body=%wide.region_5.6_spmd.clone.sunk | while | flops 337905152 | bytes 7680235 | solution.py:102
  162.2 1.2 fusion.93
  163.4 1.1 fusion.94
  164.6 1.1 fusion.95
  166.0 1.8 fusion.96
  167.9 1.2 fusion.93
  169.1 1.1 fusion.94
  170.3 1.1 fusion.95
  171.7 1.9 fusion.96
  173.7 1.2 fusion.93
  174.9 1.1 fusion.94
  176.1 1.1 fusion.95
  177.5 1.9 fusion.96
  179.5 1.2 fusion.93
  180.7 1.1 fusion.94
  181.8 1.1 fusion.95
  183.3 1.8 fusion.96
  185.2 1.2 fusion.93
  186.4 1.1 fusion.94
  187.6 1.1 fusion.95
  189.0 1.8 fusion.96
  191.0 1.2 fusion.93
  192.2 1.1 fusion.94
  193.3 1.1 fusion.95
  194.8 1.8 fusion.96
  196.7 1.2 fusion.93
  197.9 1.1 fusion.94
  199.1 1.1 fusion.95
  200.5 1.9 fusion.96
  202.5 1.2 fusion.93
  203.7 1.1 fusion.94
  204.9 1.1 fusion.95
  206.3 1.8 fusion.96
  208.2 1.2 fusion.93
  209.5 1.1 fusion.94
  210.6 1.1 fusion.95
  212.0 1.9 fusion.96
  214.0 1.2 fusion.93
  215.2 1.1 fusion.94
  216.4 1.1 fusion.95
  217.8 1.9 fusion.96
  219.7 1.1 convert_element_type.69
  220.8 6.0 all-to-all-start.4
  226.8 1.1 convert_element_type.63
  227.9 24.9 %all-to-all-done.4 = bf16[32,128,128]{2,1,0:T(8,128)(2,1)} async-done(((bf16[32,128,128]{2,1,0:T(8,128)(2,1)}), bf16[32,128,128]{2,1,0:T(8,128)(2,1)}, u32[]{:S(2)}, u32[]{:S(2)}) %all-to-all-start.4) | async-done | bytes 1048608 | tf_op jit(solution)/shard_map/all_to_all | solution.py:178
  252.7 5.8 all-to-all-start.3
  258.6 1.4 bitcast_reduce_fusion
  261.1 23.4 %all-to-all-done.3 = bf16[32,128,128]{2,1,0:T(8,128)(2,1)S(1)} async-done(((bf16[32,128,128]{2,1,0:T(8,128)(2,1)}), bf16[32,128,128]{2,1,0:T(8,128)(2,1)S(1)}, u32[]{:S(2)}, u32[]{:S(2)}) %all-to-all-start.3) | async-done | bytes 1048608 | tf_op jit(solution)/shard_map/all_to_all | solution.py:175
  287.5 229.8 %reduce-scatter.9.cloned.1.call-done = bf16[8,1024]{1,0:T(8,128)(2,1)} async-done(((bf16[128,1024]{1,0:T(8,128)(2,1)}), bf16[8,1024]{1,0:T(8,128)(2,1)}) %reduce-scatter.9.cloned.1.call-update) | async-done | bytes 16400
  517.2 0.9 copy.85
  518.9 218.4 %reduce-scatter.7.cloned.1.call-done = bf16[8,1024]{1,0:T(8,128)(2,1)} async-done(((bf16[128,1024]{1,0:T(8,128)(2,1)}), bf16[8,1024]{1,0:T(8,128)(2,1)}) %reduce-scatter.7.cloned.1.call-update) | async-done | bytes 16400
  737.3 0.9 copy.83
  (153 shorter events, 22.5 us)
Async XLA Ops:
  8.6 71.1 %all-to-all-start = ((bf16[16,8,1024]{2,1,0:T(8,128)(2,1)}), bf16[16,8,1024]{2,1,0:T(8,128)(2,1)S(1)}, u32[]{:S(2)}, u32[]{:S(2)}) async-start(bf16[16,8,1024]{2,1,0:T(8,128)(2,1)} %stack.2), calls=%async_computation | async-start | bytes 524288 | tf_op jit(solution)/shard_map/all_to_all | solution.py:114
  81.0 33.4 %all-to-all-start.2 = ((bf16[128,32,128]{2,0,1:T(8,128)(2,1)}), bf16[128,32,128]{2,0,1:T(8,128)(2,1)S(1)}, u32[]{:S(2)}, u32[]{:S(2)}) async-start(bf16[128,32,128]{2,0,1:T(8,128)(2,1)} %bitcast.6), calls=%async_computation.2 | async-start | bytes 2097152 | tf_op jit(solution)/shard_map/all_to_all | solution.py:123
  88.5 32.9 %copy-start.6 = (s32[32]{0:T(128)S(1)}, s32[32]{0:T(128)}, u32[]{:S(2)}) copy-start(s32[32]{0:T(128)} %param.13) | copy-start | bytes 388
  88.5 36.1 %copy-start.4 = (bf16[256,512]{1,0:T(8,128)(2,1)S(1)}, bf16[256,512]{1,0:T(8,128)(2,1)}, u32[]{:S(2)}) copy-start(bf16[256,512]{1,0:T(8,128)(2,1)} %param.12) | copy-start | bytes 786436
  88.6 36.4 %copy-start.5 = (bf16[256,512]{1,0:T(8,128)(2,1)S(1)}, bf16[256,512]{1,0:T(8,128)(2,1)}, u32[]{:S(2)}) copy-start(bf16[256,512]{1,0:T(8,128)(2,1)} %param.9) | copy-start | bytes 786436
  115.6 31.8 %all-to-all-start.1 = ((bf16[128,32,128]{2,0,1:T(8,128)(2,1)}), bf16[128,32,128]{2,0,1:T(8,128)(2,1)S(1)}, u32[]{:S(2)}, u32[]{:S(2)}) async-start(bf16[128,32,128]{2,0,1:T(8,128)(2,1)} %bitcast.1), calls=%async_computation.1 | async-start | bytes 2097152 | tf_op jit(solution)/shard_map/all_to_all | solution.py:122
  159.0 1.1 copy-start.1
  159.0 1.4 copy-start.2
  220.7 6.0 copy-start
  220.8 32.0 %all-to-all-start.4 = ((bf16[32,128,128]{2,1,0:T(8,128)(2,1)}), bf16[32,128,128]{2,1,0:T(8,128)(2,1)}, u32[]{:S(2)}, u32[]{:S(2)}) async-start(bf16[32,128,128]{2,1,0:T(8,128)(2,1)} %bitcast.150), calls=%async_computation.4 | async-start | bytes 2097152 | tf_op jit(solution)/shard_map/all_to_all | solution.py:178
  252.7 31.8 %all-to-all-start.3 = ((bf16[32,128,128]{2,1,0:T(8,128)(2,1)}), bf16[32,128,128]{2,1,0:T(8,128)(2,1)S(1)}, u32[]{:S(2)}, u32[]{:S(2)}) async-start(bf16[32,128,128]{2,1,0:T(8,128)(2,1)} %bitcast.149), calls=%async_computation.3 | async-start | bytes 2097152 | tf_op jit(solution)/shard_map/all_to_all | solution.py:175
  258.6 258.6 %reduce-scatter.9.cloned.1.call-start = ((), (), s32[]{:S(2)}) async-start(), calls=%async_computation.8 | async-start | bytes 278528
  260.0 25.7 %copy-start.3 = (bf16[256,4,128]{0,2,1:T(8,128)(2,1)S(1)}, bf16[256,4,128]{0,2,1:T(8,128)(2,1)}, u32[]{:S(2)}) copy-start(bf16[256,4,128]{0,2,1:T(8,128)(2,1)} %get-tuple-element.348) | copy-start | bytes 786436
  261.1 476.2 %reduce-scatter.7.cloned.1.call-start = ((), (), s32[]{:S(2)}) async-start(), calls=%async_computation.7 | async-start | bytes 278528
Sparse Core Ops, SparseCore 0:
  263.8 253.3 reduce-scatter.8
  521.7 215.5 reduce-scatter.6
